TPU v7x, 32 devices: a whole 2x2x4 slice. The times are simulated.
32 devices in a mesh: replica: 4 (over y, core), kvhead: 4 (over z), ffn: 2 (over x).
Axes of the slice: x: 2, y: 2, z: 4, core: 2. Of those that a mesh axis runs over, the one named last changes fastest.
Arguments:
- queries: bfloat16 [16, 16384], P('replica', 'kvhead'), may hold values from -400 to 400
- k_cache: bfloat16 [512, 64, 1024], P(('replica', 'ffn'), None, 'kvhead'), may hold values from -6 to 6
- v_cache: bfloat16 [512, 64, 1024], P(('replica', 'ffn'), None, 'kvhead'), may hold values from -6 to 6
- page_table: int32 [16, 32], P('replica', 'ffn'), may hold values from 0 to 63, as said below
- seq_lens: int32 [16], P('replica'), may hold values from 1 to 2048, as said below
- out_proj: bfloat16 [16384, 16384], P('kvhead', ('replica', 'ffn')), may hold values from -0.125 to 0.125
- residual: bfloat16 [16, 16384], P('kvhead', ('replica', 'ffn')), may hold values from -40 to 40
- norm_gain: bfloat16 [16384], P(('replica', 'ffn')), may hold values from 0.099609375 to 1.8984375
- gate_weight: bfloat16 [26624, 16384], P(('replica', 'kvhead', 'ffn')), may hold values from -0.046875 to 0.046875
- up_weight: bfloat16 [26624, 16384], P(('replica', 'kvhead', 'ffn')), may hold values from -0.046875 to 0.046875
Outputs:
- post_attn: bfloat16 [16, 16384], P('kvhead', ('replica', 'ffn'))
- hidden: bfloat16 [16, 26624], P(None, ('replica', 'kvhead', 'ffn'))
Inputs may be any that keep to these rules, and one draw needn't show every extreme that they name: `page_table`: over the 4 rows of one replica, the entries of page columns j with the same j // 16 name every pool page 0 to 63 exactly once. `seq_lens`: some row has length 2048.
All inputs are finite; a program needn't handle non-finite values.
Results may differ from a plain program's by a relative error of at most 0.0079.
Values may be sent and summed in bfloat16 or wider, within the bound.
A program may use at most 192 MiB of HBM per device.

v0:
```python
import math
import jax
import jax.numpy as jnp
from jax import lax
from jax.sharding import PartitionSpec as P

D = 16384
HD = 128
GQ = 16
NEG_FILL = -1e30
NORM_EPS = 1e-05


def merged(part, axis, combine):
    gathered = jax.tree.map(lambda a: lax.all_gather(a, axis), part)

    def take(source):
        return jax.tree.map(lambda a: lax.dynamic_index_in_dim(a, source, 0, False), gathered)

    return lax.fori_loop(
        1, lax.axis_size(axis), lambda source, state: combine(state, take(source)), take(0)
    )


def join_parts(earlier, later):
    first_max, first_total, first_out = earlier
    second_max, second_total, second_out = later
    overall = jnp.maximum(first_max, second_max)
    first_factor = jnp.exp(first_max - overall)
    second_factor = jnp.exp(second_max - overall)
    joined_total = first_total * first_factor + second_total * second_factor
    joined_out = first_out * first_factor[..., None] + second_out * second_factor[..., None]
    return (overall, joined_total, joined_out)


def per_device(
    queries,
    k_cache,
    v_cache,
    page_table,
    seq_lens,
    out_proj,
    residual,
    norm_gain,
    gate_weight,
    up_weight,
):
    score_scale = 1.0 / math.sqrt(HD)
    row_count = queries.shape[0]
    local_heads = k_cache.shape[2] // HD
    span_len = page_table.shape[1] * k_cache.shape[1]
    key_rows = k_cache[page_table].reshape(row_count, span_len, local_heads, HD)
    value_rows = v_cache[page_table].reshape(row_count, span_len, local_heads, HD)
    query_heads = queries.reshape(row_count, local_heads, GQ, HD)
    scores = (
        jnp.einsum("rkgd,rskd->rkgs", query_heads, key_rows, preferred_element_type=jnp.float32)
        * score_scale
    )
    positions = lax.axis_index("ffn") * span_len + jnp.arange(span_len, dtype=jnp.int32)
    visible = (positions[None, :] < seq_lens[:, None])[:, None, None, :]
    block_max = jnp.max(jnp.where(visible, scores, NEG_FILL), axis=-1)
    weights = jnp.where(visible, jnp.exp(scores - block_max[..., None]), 0.0)
    block_total = jnp.sum(weights, axis=-1)
    block_out = jnp.einsum(
        "rkgs,rskd->rkgd",
        weights.astype(jnp.bfloat16),
        value_rows,
        preferred_element_type=jnp.float32,
    )
    overall, denominator, weighted = merged((block_max, block_total, block_out), "ffn", join_parts)
    contexts = (
        (weighted / denominator[..., None])
        .astype(jnp.bfloat16)
        .reshape(row_count, local_heads * GQ * HD)
    )
    partial_value = jnp.dot(
        lax.all_gather(contexts, "replica", axis=0, tiled=True),
        out_proj,
        preferred_element_type=jnp.float32,
    )
    own_count = residual.shape[0]
    own_first = lax.axis_index("kvhead") * own_count
    own_part = lax.dynamic_slice_in_dim(partial_value, own_first, own_count, 0) + residual.astype(
        jnp.float32
    )
    partial_value = lax.dynamic_update_slice_in_dim(partial_value, own_part, own_first, 0)
    gain_wide = norm_gain.astype(jnp.float32)
    summed = lax.psum(partial_value, "kvhead")
    post_all = summed.astype(jnp.bfloat16)
    post_attn = lax.dynamic_slice_in_dim(post_all, own_first, own_count, 0)
    widened = post_all.astype(jnp.float32)
    squares = lax.psum(jnp.sum(widened * widened, axis=1), ("replica", "ffn"))
    normed = (widened * lax.rsqrt(squares / D + NORM_EPS)[:, None] * gain_wide).astype(jnp.bfloat16)
    contract = (((1,), (1,)), ((), ()))
    shard_cols = lax.all_gather(normed, ("replica", "ffn"), axis=1, tiled=True)
    gate_sum = lax.dot_general(
        shard_cols, gate_weight, contract, preferred_element_type=jnp.float32
    )
    up_sum = lax.dot_general(shard_cols, up_weight, contract, preferred_element_type=jnp.float32)
    hidden = (jax.nn.silu(gate_sum) * up_sum).astype(jnp.bfloat16)
    return (post_attn, hidden)


def solution(mesh):
    in_specs = (
        P("replica", "kvhead"),
        P(("replica", "ffn"), None, "kvhead"),
        P(("replica", "ffn"), None, "kvhead"),
        P("replica", "ffn"),
        P("replica"),
        P("kvhead", ("replica", "ffn")),
        P("kvhead", ("replica", "ffn")),
        P(("replica", "ffn")),
        P(("replica", "kvhead", "ffn"), None),
        P(("replica", "kvhead", "ffn"), None),
    )
    out_specs = (P("kvhead", ("replica", "ffn")), P(None, ("replica", "kvhead", "ffn")))
    return jax.shard_map(
        per_device, mesh=mesh, in_specs=in_specs, out_specs=out_specs, check_vma=False
    )
```

profile of v0, /device:TPU:1, one launch (start us, length us, event | category | flops | bytes accessed | tf_op | source)
XLA Modules:
  0.0 121.5 jit_solution(7688263210400951377)
XLA Ops:
  0.7 0.9 broadcast_compare_fusion
  1.5 0.7 compare_select_fusion
  2.2 0.1 reshape.100
  2.3 2.0 %gather_fusion = bf16[64,64,256]{2,1,0:T(8,128)(2,1)} fusion(bf16[64,64,256]{2,1,0:T(8,128)(2,1)S(1)} %copy-done, s32[1024]{0:T(1024)S(1)} %pad_clamp_fusion), kind=kCustom, calls=%fused_computation | custom fusion | bytes 4194560 | tf_op jit(solution)/shard_map/gather | solution.py:52
  4.4 2.6 %reshape.95 = bf16[4,1024,2,128]{3,2,1,0:T(2,128)(2,1)S(1)} reshape(bf16[64,64,256]{2,1,0:T(8,128)(2,1)} %gather_fusion) | data formatting | bytes 4194304 | tf_op jit(solution)/shard_map/reshape | solution.py:52
  6.9 0.7 select_reduce_fusion
  7.7 0.3 bitcast_reduce_fusion
  7.9 3.8 %all-gather.2 = f32[8,2,16]{2,1,0:T(2,128)S(1)} all-gather(f32[4,2,16]{2,1,0:T(2,128)S(1)} %bitcast_reduce_fusion), channel_id=4, replica_groups=mesh['replica'=4,'kvhead'=4,'ffn'=2] {'ffn'}, dimensions={0}, use_global_device_ids=true | all-gather | bytes 1536 | tf_op jit(solution)/shard_map/all_gather | solution.py:15
  11.7 3.2 %all-gather.1 = f32[8,2,16]{2,1,0:T(2,128)S(1)} all-gather(f32[4,2,16]{2,1,0:T(2,128)S(1)} %get-tuple-element.21), channel_id=3, replica_groups=mesh['replica'=4,'kvhead'=4,'ffn'=2] {'ffn'}, dimensions={0}, use_global_device_ids=true | all-gather | bytes 1536 | tf_op jit(solution)/shard_map/all_gather | solution.py:15
  14.9 2.3 %gather_fusion.1 = bf16[64,64,256]{2,1,0:T(8,128)(2,1)S(1)} fusion(bf16[64,64,256]{2,1,0:T(8,128)(2,1)} %param.12, s32[1024]{0:T(1024)S(1)} %pad_clamp_fusion), kind=kCustom, calls=%fused_computation.1 | custom fusion | bytes 4194560 | tf_op jit(solution)/shard_map/gather | solution.py:53
  17.2 2.1 %reshape.97 = bf16[4,1024,2,128]{3,2,1,0:T(2,128)(2,1)} reshape(bf16[64,64,256]{2,1,0:T(8,128)(2,1)S(1)} %gather_fusion.1) | data formatting | bytes 4194304 | tf_op jit(solution)/shard_map/reshape | solution.py:53
  19.3 2.0 %fusion = f32[4,2,16,128]{3,2,1,0:T(8,128)S(1)} fusion(bf16[4,1024,2,128]{3,2,1,0:T(2,128)(2,1)} %reshape.97, f32[4,2,1024,16]{2,3,1,0:T(8,128)S(1)} %get-tuple-element.22, f32[4,2,16]{2,1,0:T(2,128)S(1)} %get-tuple-element.21, pred[4,1024]{1,0:T(4,128)(4,1)S(1)} %broadcast_compare_fusion), kind=kOutput, calls=%fused_computation.2 | convolution fusion | flops 33947648 | bytes 2691584 | tf_op jit(solution)/shard_map/rkgs,rskd->rkgd/dot_general | solution.py:64
  21.3 3.8 %all-gather = f32[8,2,16,128]{3,2,1,0:T(8,128)S(1)} all-gather(f32[4,2,16,128]{3,2,1,0:T(8,128)S(1)} %fusion), channel_id=2, replica_groups=mesh['replica'=4,'kvhead'=4,'ffn'=2] {'ffn'}, dimensions={0}, use_global_device_ids=true | all-gather | bytes 196608 | tf_op jit(solution)/shard_map/all_gather | solution.py:15
  25.1 0.1 fusion.16
  25.3 9.3 %all-gather.3 = bf16[4,4,4096]{2,1,0:T(4,128)(2,1)S(1)} all-gather(bf16[1,4,4096]{2,1,0:T(4,128)(2,1)S(1)} %reshape.139), channel_id=1, replica_groups=mesh['replica'=4,'kvhead'=4,'ffn'=2] {'replica'}, dimensions={0}, use_global_device_ids=true | all-gather | bytes 163840 | tf_op jit(solution)/shard_map/all_gather | solution.py:77
  34.6 8.1 %fusion.23 = f32[16,2048]{1,0:T(8,128)S(1)} fusion(bf16[16,4096]{1,0:T(8,128)(2,1)S(1)} %reshape.140, bf16[4096,2048]{1,0:T(8,128)(2,1)} %param.15), kind=kOutput, calls=%fused_computation.41 | convolution fusion | flops 268435456 | bytes 17039360 | tf_op jit(solution)/shard_map/dot_general | solution.py:76
  42.7 17.8 %all-reduce.1 = bf16[16,2048]{1,0:T(8,128)(2,1)S(1)} all-reduce(f32[16,2048]{1,0:T(8,128)S(1)} %add_dynamic-update-slice_fusion), channel_id=1, replica_groups=mesh['replica'=4,'kvhead'=4,'ffn'=2] {'kvhead'}, use_global_device_ids=true, to_apply=%region_2.3 | all-reduce | flops 32768 | bytes 196608 | tf_op jit(solution)/shard_map/psum | solution.py:88
  60.5 0.1 fusion.11
  60.6 17.2 %psum.15 = f32[16]{0:T(128)S(1)} all-reduce(f32[16]{0:T(128)S(1)} %fusion.11), channel_id=1, replica_groups=mesh['replica'=4,'kvhead'=4,'ffn'=2] {'replica','ffn'}, use_global_device_ids=true, to_apply=%region_4.5 | all-reduce | flops 16 | bytes 128 | tf_op jit(solution)/shard_map/psum | solution.py:92
  77.8 0.1 fusion.13
  77.9 17.4 %all_gather.31 = bf16[16,16384]{1,0:T(8,128)(2,1)S(1)} all-gather(bf16[16,2048]{1,0:T(8,128)(2,1)S(1)} %fusion.13), channel_id=1, replica_groups=mesh['replica'=4,'kvhead'=4,'ffn'=2] {'replica','ffn'}, dimensions={1}, use_global_device_ids=true | all-gather | bytes 589824 | tf_op jit(solution)/shard_map/all_gather | solution.py:95
  95.3 12.4 %fusion.24 = f32[16,832]{1,0:T(8,128)S(1)} fusion(bf16[16,16384]{1,0:T(8,128)(2,1)S(1)} %all_gather.31, bf16[832,16384]{1,0:T(8,128)(2,1)} %param.18), kind=kOutput, calls=%fused_computation.42 | convolution fusion | flops 436207616 | bytes 27840512 | tf_op jit(solution)/shard_map/dot_general | solution.py:96
  107.7 13.2 %fusion.7 = bf16[16,832]{1,0:T(8,128)(2,1)} fusion(bf16[16,16384]{1,0:T(8,128)(2,1)S(1)} %all_gather.31, bf16[832,16384]{1,0:T(8,128)(2,1)} %param.19, f32[16,832]{1,0:T(8,128)S(1)} %fusion.24), kind=kOutput, calls=%fused_computation.8 | convolution fusion | flops 436287488 | bytes 27867136 | tf_op jit(solution)/shard_map/dot_general | solution.py:99
  120.9 0.6 constant_dynamic-slice_fusion
  (19 shorter events, 0.2 us)
Async XLA Ops:
  0.6 1.7 %copy-start = (bf16[64,64,256]{2,1,0:T(8,128)(2,1)S(1)}, bf16[64,64,256]{2,1,0:T(8,128)(2,1)}, u32[]{:S(2)}) copy-start(bf16[64,64,256]{2,1,0:T(8,128)(2,1)} %param.11) | copy-start | bytes 6291460
  4.4 2.6 %copy-start.2 = (bf16[4,4096]{1,0:T(4,128)(2,1)S(1)}, bf16[4,4096]{1,0:T(4,128)(2,1)}, u32[]{:S(2)}) copy-start(bf16[4,4096]{1,0:T(4,128)(2,1)} %param.10) | copy-start | bytes 98308
  34.6 8.1 %copy-start.3 = (bf16[4,2048]{1,0:T(4,128)(2,1)S(1)}, bf16[4,2048]{1,0:T(4,128)(2,1)}, u32[]{:S(2)}) copy-start(bf16[4,2048]{1,0:T(4,128)(2,1)} %param.16) | copy-start | bytes 49156
  34.6 43.2 %copy-start.4 = (bf16[2048]{0:T(1024)(128)(2,1)S(1)}, bf16[2048]{0:T(1024)(128)(2,1)}, u32[]{:S(2)}) copy-start(bf16[2048]{0:T(1024)(128)(2,1)} %param.17) | copy-start | bytes 12292
  107.7 13.8 %copy-start.1 = (bf16[64,64,256]{2,1,0:T(8,128)(2,1)S(1)}, bf16[64,64,256]{2,1,0:T(8,128)(2,1)}, u32[]{:S(2)}) copy-start(bf16[64,64,256]{2,1,0:T(8,128)(2,1)} %param.11) | copy-start | bytes 6291460
where the time goes:
time: 122 us; the launch traced here: 121 us
  blocking collectives  72.4 us (59%)
  matrix products  36.4 us (30%)
  local copies, waits for them, and re-layouts  9.74 us (8%)
  other arithmetic  2.21 us (2%)
    psum x1, blocking collectives, per_device(): summed = lax.psum(partial_value, 'kvhead')  17.8 us
    all_gather x1, blocking collectives, per_device(): shard_cols = lax.all_gather(normed, ('replica', 'ffn'), axis=1, tiled=True)  17.4 us
    psum x1, blocking collectives, per_device(): squares = lax.psum(jnp.sum(widened * widened, axis=1), ('replica', 'ffn'))  17.2 us
    dot_general x1, matrix products, per_device(): lax.dot_general(shard_cols, up_weight, contract, preferred_element_type=j...  13.2 us
    dot_general x1, matrix products, per_device(): lax.dot_general(shard_cols, gate_weight, contract, preferred_element_type...  12.4 us
    all_gather x3, blocking collectives, merged(): gathered = jax.tree.map(lambda a: lax.all_gather(a, axis), part)  10.7 us
    all_gather x1, blocking collectives, per_device(): lax.all_gather(contexts, 'replica', axis=0, tiled=True)  9.29 us
    dot_general x1, matrix products, per_device(): jnp.dot(lax.all_gather(contexts, 'replica', axis=0, tiled=True), out_proj...  8.05 us

commit v1 on v0

--- a/solution.py
+++ b/solution.py
@@ -3,6 +3,7 @@
 import jax.numpy as jnp
 from jax import lax
 from jax.sharding import PartitionSpec as P
+from jax.lax import axis_size, ppermute
 
 D = 16384
 HD = 128
@@ -85,7 +86,17 @@
     )
     partial_value = lax.dynamic_update_slice_in_dim(partial_value, own_part, own_first, 0)
     gain_wide = norm_gain.astype(jnp.float32)
-    summed = lax.psum(partial_value, "kvhead")
+
+    def floor_write(array_in, named_axis):
+        n_dev_all = axis_size(named_axis)
+        z2 = lambda high: [(h, h ^ high) for h in range(n_dev_all)]
+        new = array_in
+        for nth in range(n_dev_all.bit_length() - 1):
+            front = z2(1 << nth)
+            new = new + ppermute(new, axis_name=named_axis, perm=front)
+        return new
+
+    summed = floor_write(partial_value, "kvhead")
     post_all = summed.astype(jnp.bfloat16)
     post_attn = lax.dynamic_slice_in_dim(post_all, own_first, own_count, 0)
     widened = post_all.astype(jnp.float32)

time: 122 us -> 115 us (0.943)
  blocking collectives: 72.4 us -> 51.8 us
  waiting for transfers between devices: 0 us -> 9.46 us
  starting transfers between devices: 0 us -> 4.07 us
    psum x1 -> x0, blocking collectives: 17.8 us -> none  [per_device(): summed = lax.psum(partial_value, 'kvhead')]
    ppermute x0 -> x2, waiting for transfers between devices: none -> 9.46 us  [floor_write(): new = new + ppermute(new, axis_name=named_axis, perm=front)]
    ppermute x0 -> x2, starting transfers between devices: none -> 4.07 us  [floor_write(): new = new + ppermute(new, axis_name=named_axis, perm=front)]
    psum x1, blocking collectives: 17.2 us -> 14.4 us  [per_device(): squares = lax.psum(jnp.sum(widened * widened, axis=1), ('replica', 'ffn'))]
  transfers between devices with their start and end apart: 0 -> 2, of which waited for: 0 -> 2; matrix products, arithmetic and copies ran while one was open for 0% -> 0% of each run, Pallas kernels for 0% -> 0%
where the time goes in v1:
time: 115 us; the launch traced here: 114 us
  blocking collectives  51.8 us (45%)
  matrix products  36.4 us (32%)
  local copies, waits for them, and re-layouts  10.4 us (9%)
  waiting for transfers between devices  9.46 us (8%)
  starting transfers between devices  4.07 us (4%)
  other arithmetic  1.56 us (1%)
    all_gather x1, blocking collectives, per_device(): shard_cols = lax.all_gather(normed, ('replica', 'ffn'), axis=1, tiled=True)  17.4 us
    psum x1, blocking collectives, per_device(): squares = lax.psum(jnp.sum(widened * widened, axis=1), ('replica', 'ffn'))  14.4 us
    dot_general x1, matrix products, per_device(): lax.dot_general(shard_cols, up_weight, contract, preferred_element_type=j...  13.2 us
    dot_general x1, matrix products, per_device(): lax.dot_general(shard_cols, gate_weight, contract, preferred_element_type...  12.4 us
    all_gather x3, blocking collectives, merged(): gathered = jax.tree.map(lambda a: lax.all_gather(a, axis), part)  10.7 us
    ppermute x2, waiting for transfers between devices, floor_write(): new = new + ppermute(new, axis_name=named_axis, perm=front)  9.46 us
    all_gather x1, blocking collectives, per_device(): lax.all_gather(contexts, 'replica', axis=0, tiled=True)  9.29 us
    dot_general x1, matrix products, per_device(): jnp.dot(lax.all_gather(contexts, 'replica', axis=0, tiled=True), out_proj...  8.05 us
  transfers between devices with their start and end apart: 2, of which 2 were waited for; matrix products, arithmetic and copies ran while one was open for 0% of the time, Pallas kernels for 0%

profile of v1, /device:TPU:1, one launch (start us, length us, event | category | flops | bytes accessed | tf_op | source)
XLA Modules:
  0.0 114.5 jit_solution(1354989917903433492)
XLA Ops:
  0.7 0.8 compare_select_fusion
  1.6 0.7 copy-done
  2.2 2.0 %gather_fusion = bf16[64,64,256]{2,1,0:T(8,128)(2,1)} fusion(bf16[64,64,256]{2,1,0:T(8,128)(2,1)S(1)} %copy-done, s32[1024]{0:T(1024)S(1)} %pad_clamp_fusion), kind=kCustom, calls=%fused_computation | custom fusion | bytes 4194560 | tf_op jit(solution)/shard_map/gather | solution.py:53
  4.3 2.6 %reshape.95 = bf16[4,1024,2,128]{3,2,1,0:T(2,128)(2,1)S(1)} reshape(bf16[64,64,256]{2,1,0:T(8,128)(2,1)} %gather_fusion) | data formatting | bytes 4194304 | tf_op jit(solution)/shard_map/reshape | solution.py:53
  7.0 0.7 select_reduce_fusion
  7.7 3.8 %all-gather.1 = f32[8,2,16]{2,1,0:T(2,128)S(1)} all-gather(f32[4,2,16]{2,1,0:T(2,128)S(1)} %get-tuple-element.23), channel_id=3, replica_groups=mesh['replica'=4,'kvhead'=4,'ffn'=2] {'ffn'}, dimensions={0}, use_global_device_ids=true | all-gather | bytes 1536 | tf_op jit(solution)/shard_map/all_gather | solution.py:16
  11.5 0.2 bitcast_reduce_fusion
  11.7 3.2 %all-gather.2 = f32[8,2,16]{2,1,0:T(2,128)S(1)} all-gather(f32[4,2,16]{2,1,0:T(2,128)S(1)} %bitcast_reduce_fusion), channel_id=4, replica_groups=mesh['replica'=4,'kvhead'=4,'ffn'=2] {'ffn'}, dimensions={0}, use_global_device_ids=true | all-gather | bytes 1536 | tf_op jit(solution)/shard_map/all_gather | solution.py:16
  14.9 2.3 %gather_fusion.1 = bf16[64,64,256]{2,1,0:T(8,128)(2,1)S(1)} fusion(bf16[64,64,256]{2,1,0:T(8,128)(2,1)} %param.12, s32[1024]{0:T(1024)S(1)} %pad_clamp_fusion), kind=kCustom, calls=%fused_computation.1 | custom fusion | bytes 4194560 | tf_op jit(solution)/shard_map/gather | solution.py:54
  17.2 2.1 %reshape.97 = bf16[4,1024,2,128]{3,2,1,0:T(2,128)(2,1)} reshape(bf16[64,64,256]{2,1,0:T(8,128)(2,1)S(1)} %gather_fusion.1) | data formatting | bytes 4194304 | tf_op jit(solution)/shard_map/reshape | solution.py:54
  19.3 2.0 %fusion = f32[4,2,16,128]{3,2,1,0:T(8,128)S(1)} fusion(bf16[4,1024,2,128]{3,2,1,0:T(2,128)(2,1)} %reshape.97, f32[4,2,1024,16]{2,3,1,0:T(8,128)S(1)} %get-tuple-element.32, f32[4,2,16]{2,1,0:T(2,128)S(1)} %get-tuple-element.23, pred[4,1024]{1,0:T(4,128)(4,1)S(1)} %broadcast_compare_fusion), kind=kOutput, calls=%fused_computation.2 | convolution fusion | flops 33947648 | bytes 2691584 | tf_op jit(solution)/shard_map/rkgs,rskd->rkgd/dot_general | solution.py:65
  21.3 3.8 %all-gather = f32[8,2,16,128]{3,2,1,0:T(8,128)S(1)} all-gather(f32[4,2,16,128]{3,2,1,0:T(8,128)S(1)} %fusion), channel_id=2, replica_groups=mesh['replica'=4,'kvhead'=4,'ffn'=2] {'ffn'}, dimensions={0}, use_global_device_ids=true | all-gather | bytes 196608 | tf_op jit(solution)/shard_map/all_gather | solution.py:16
  25.3 9.3 %all-gather.3 = bf16[4,4,4096]{2,1,0:T(4,128)(2,1)S(1)} all-gather(bf16[1,4,4096]{2,1,0:T(4,128)(2,1)S(1)} %reshape.139), channel_id=1, replica_groups=mesh['replica'=4,'kvhead'=4,'ffn'=2] {'replica'}, dimensions={0}, use_global_device_ids=true | all-gather | bytes 163840 | tf_op jit(solution)/shard_map/all_gather | solution.py:78
  34.6 8.1 %fusion.23 = f32[16,2048]{1,0:T(8,128)S(1)} fusion(bf16[16,4096]{1,0:T(8,128)(2,1)S(1)} %reshape.140, bf16[4096,2048]{1,0:T(8,128)(2,1)} %param.15), kind=kOutput, calls=%fused_computation.42 | convolution fusion | flops 268435456 | bytes 17039360 | tf_op jit(solution)/shard_map/dot_general | solution.py:77
  42.7 1.7 %collective-permute-start = (f32[16,2048]{1,0:T(8,128)S(1)}, f32[16,2048]{1,0:T(8,128)S(1)}, u32[]{:S(2)}, u32[]{:S(2)}) collective-permute-start(f32[16,2048]{1,0:T(8,128)S(1)} %add_dynamic-update-slice_fusion), channel_id=1, source_target_pairs={{0,2},{2,0},{4,6},{6,4},{1,3},{3,1},{5,7},{7,5},{8,10},{10,8},{12,... | collective-permute-start | bytes 393224 | tf_op jit(solution)/shard_map/ppermute | solution.py:96
  44.4 3.6 %collective-permute-done = f32[16,2048]{1,0:T(8,128)S(1)} collective-permute-done((f32[16,2048]{1,0:T(8,128)S(1)}, f32[16,2048]{1,0:T(8,128)S(1)}, u32[]{:S(2)}, u32[]{:S(2)}) %collective-permute-start) | collective-permute-done | bytes 131104 | tf_op jit(solution)/shard_map/ppermute | solution.py:96
  48.1 2.4 %collective-permute-start.1 = (f32[16,2048]{1,0:T(8,128)S(1)}, f32[16,2048]{1,0:T(8,128)S(1)}, u32[]{:S(2)}, u32[]{:S(2)}) collective-permute-start(f32[16,2048]{1,0:T(8,128)S(1)} %add.70), channel_id=1, source_target_pairs={{0,4},{2,6},{4,0},{6,2},{1,5},{3,7},{5,1},{7,3},{8,12},{10,14},{12... | collective-permute-start | bytes 393224 | tf_op jit(solution)/shard_map/ppermute | solution.py:96
  50.4 5.8 %collective-permute-done.1 = f32[16,2048]{1,0:T(8,128)S(1)} collective-permute-done((f32[16,2048]{1,0:T(8,128)S(1)}, f32[16,2048]{1,0:T(8,128)S(1)}, u32[]{:S(2)}, u32[]{:S(2)}) %collective-permute-start.1) | collective-permute-done | bytes 131104 | tf_op jit(solution)/shard_map/ppermute | solution.py:96
  56.3 0.1 fusion.11
  56.4 14.4 %psum.7 = f32[16]{0:T(128)S(1)} all-reduce(f32[16]{0:T(128)S(1)} %get-tuple-element.18), channel_id=1, replica_groups=mesh['replica'=4,'kvhead'=4,'ffn'=2] {'replica','ffn'}, use_global_device_ids=true, to_apply=%region_3.4 | all-reduce | flops 16 | bytes 128 | tf_op jit(solution)/shard_map/psum | solution.py:103
  70.8 0.6 constant_dynamic-slice_fusion
  71.5 17.4 %all_gather.31 = bf16[16,16384]{1,0:T(8,128)(2,1)S(1)} all-gather(bf16[16,2048]{1,0:T(8,128)(2,1)S(1)} %fusion.13), channel_id=1, replica_groups=mesh['replica'=4,'kvhead'=4,'ffn'=2] {'replica','ffn'}, dimensions={1}, use_global_device_ids=true | all-gather | bytes 589824 | tf_op jit(solution)/shard_map/all_gather | solution.py:106
  88.9 12.4 %fusion.24 = f32[16,832]{1,0:T(8,128)S(1)} fusion(bf16[16,16384]{1,0:T(8,128)(2,1)S(1)} %all_gather.31, bf16[832,16384]{1,0:T(8,128)(2,1)} %param.18), kind=kOutput, calls=%fused_computation.43 | convolution fusion | flops 436207616 | bytes 27840512 | tf_op jit(solution)/shard_map/dot_general | solution.py:107
  101.3 13.2 %fusion.7 = bf16[16,832]{1,0:T(8,128)(2,1)} fusion(bf16[16,16384]{1,0:T(8,128)(2,1)S(1)} %all_gather.31, bf16[832,16384]{1,0:T(8,128)(2,1)} %param.19, f32[16,832]{1,0:T(8,128)S(1)} %fusion.24), kind=kOutput, calls=%fused_computation.8 | convolution fusion | flops 436287488 | bytes 27867136 | tf_op jit(solution)/shard_map/dot_general | solution.py:110
  (25 shorter events, 0.5 us)
Async XLA Ops:
  0.6 1.6 %copy-start = (bf16[64,64,256]{2,1,0:T(8,128)(2,1)S(1)}, bf16[64,64,256]{2,1,0:T(8,128)(2,1)}, u32[]{:S(2)}) copy-start(bf16[64,64,256]{2,1,0:T(8,128)(2,1)} %param.11) | copy-start | bytes 6291460
  4.3 2.6 %copy-start.2 = (bf16[4,4096]{1,0:T(4,128)(2,1)S(1)}, bf16[4,4096]{1,0:T(4,128)(2,1)}, u32[]{:S(2)}) copy-start(bf16[4,4096]{1,0:T(4,128)(2,1)} %param.10) | copy-start | bytes 98308
  4.3 2.6 %copy-start.5 = (s32[4]{0:T(128)S(1)}, s32[4]{0:T(128)}, u32[]{:S(2)}) copy-start(s32[4]{0:T(128)} %param.14) | copy-start | bytes 52
  34.6 8.1 %copy-start.3 = (bf16[4,2048]{1,0:T(4,128)(2,1)S(1)}, bf16[4,2048]{1,0:T(4,128)(2,1)}, u32[]{:S(2)}) copy-start(bf16[4,2048]{1,0:T(4,128)(2,1)} %param.16) | copy-start | bytes 49156
  34.6 15.8 %copy-start.4 = (bf16[2048]{0:T(1024)(128)(2,1)S(1)}, bf16[2048]{0:T(1024)(128)(2,1)}, u32[]{:S(2)}) copy-start(bf16[2048]{0:T(1024)(128)(2,1)} %param.17) | copy-start | bytes 12292
  42.7 5.3 %collective-permute-start = (f32[16,2048]{1,0:T(8,128)S(1)}, f32[16,2048]{1,0:T(8,128)S(1)}, u32[]{:S(2)}, u32[]{:S(2)}) collective-permute-start(f32[16,2048]{1,0:T(8,128)S(1)} %add_dynamic-update-slice_fusion), channel_id=1, source_target_pairs={{0,2},{2,0},{4,6},{6,4},{1,3},{3,1},{5,7},{7,5},{8,10},{10,8},{12,... | collective-permute-start | bytes 393224 | tf_op jit(solution)/shard_map/ppermute | solution.py:96
  48.1 8.2 %collective-permute-start.1 = (f32[16,2048]{1,0:T(8,128)S(1)}, f32[16,2048]{1,0:T(8,128)S(1)}, u32[]{:S(2)}, u32[]{:S(2)}) collective-permute-start(f32[16,2048]{1,0:T(8,128)S(1)} %add.70), channel_id=1, source_target_pairs={{0,4},{2,6},{4,0},{6,2},{1,5},{3,7},{5,1},{7,3},{8,12},{10,14},{12... | collective-permute-start | bytes 393224 | tf_op jit(solution)/shard_map/ppermute | solution.py:96
  101.3 13.2 %copy-start.1 = (bf16[64,64,256]{2,1,0:T(8,128)(2,1)S(1)}, bf16[64,64,256]{2,1,0:T(8,128)(2,1)}, u32[]{:S(2)}) copy-start(bf16[64,64,256]{2,1,0:T(8,128)(2,1)} %param.11) | copy-start | bytes 6291460
